TPU v7x, 512 devices: a whole 4x8x8 slice. The times are simulated.
512 devices in a mesh: mod: 512 (over y, z, x, core).
Axes of the slice: x: 4, y: 8, z: 8, core: 2. Of those that a mesh axis runs over, the one named last changes fastest.
Arguments:
- loads: bfloat16 [32, 524288], P(None, 'mod')
- modes: float32 [6, 524288], P(None, 'mod'), may hold values from -0.6 to 0.6
- pinv: bfloat16 [524288, 1024], P('mod')
- schur: bfloat16 [524288, 1024], P('mod')
- coarse_inverse: float32 [3072, 3072], P('mod')
- connectors: int32 [512, 3, 8], P('mod'), may hold values from -1 to 4, as said below
Outputs:
- multipliers: float32 [32, 524288], P(None, 'mod')
Inputs may be any that keep to these rules, and one draw needn't show every extreme that they name: connectors[s, 0, b] is 0 for an unused block, or 1, 2, 3, 4 when the block is tied to module s + 1, s - 1, s + 8, s - 8; its partner is the block of that module with the opposite direction (1 with 2, 3 with 4) and the same slot connectors[s, 1, b], which is below 2 (0 on unused blocks). connectors[s, 2, b] is +1 or -1 on used blocks, opposite at the two ends of a connector, and 0 on unused ones. Partners stay within rows of 8 modules along the first kind of direction and within the modules along the second. A module uses at most 2 blocks towards one neighbour, and some module uses 2.
All inputs are finite; a program needn't handle non-finite values.
Results may differ from a plain program's by a relative error of at most 0.0015.
Values sent between devices are 32-bit elements; how exact they have to be, the bound alone decides.
A program may use at most 64 MiB of HBM per device.

v0:
```python
import jax
import jax.numpy as jnp
from jax import lax
from jax.sharding import PartitionSpec as P

MODES = 6
MAXC = 2
ACROSS = 8
highest = lax.Precision.HIGHEST


def shifted(block, axis, distance):
    devices = range(lax.axis_size(axis))
    route = [(i - distance, i) for i in devices if i - distance in devices]
    return lax.ppermute(block, axis, route)


def on_device(loads, modes, pinv, schur, coarse_inverse, connectors):
    case_count, dof_count = loads.shape
    block_count = connectors.shape[2]
    block_size = dof_count // block_count
    orient = connectors[0, 2].astype(jnp.float32)
    orient_flat = jnp.repeat(orient, block_size)[None, :]
    headings = connectors[0, 0]
    slot_ids = connectors[0, 1]
    heading_ids = jnp.arange(4, dtype=jnp.int32)[:, None, None] + 1
    slot_range = jnp.arange(MAXC, dtype=jnp.int32)[None, :, None]
    selector = (
        (headings[None, None] == heading_ids) & (slot_ids[None, None] == slot_range)
    ).astype(jnp.float32)
    offsets = [1, -1, ACROSS, -ACROSS]
    module_count = coarse_inverse.shape[1] // MODES
    inverse_view = coarse_inverse.reshape(MODES, module_count, MODES)

    def jump_with(values_in, mover):
        signed = values_in.reshape(case_count, block_count, block_size) * orient[None, :, None]
        summed = signed
        for heading in range(4):
            packed = jnp.einsum("kb,cbe->kce", selector[heading ^ 1], signed, precision=highest)
            received = mover(packed, heading)
            summed = summed + jnp.einsum(
                "kb,kce->cbe", selector[heading], received, precision=highest
            )
        return summed.reshape(case_count, dof_count)

    def move_values(packed, heading):
        return shifted(packed, "mod", -offsets[heading])

    def move_lifted(packed, heading):
        return shifted(packed, "mod", -offsets[heading])

    def apply_jump(values_in):
        return jump_with(values_in, move_values)

    def coarse_rhs(values_in):
        return lax.dot_general(modes, values_in, (((1,), (1,)), ((), ())), precision=highest)

    def lift(amplitude):
        return lax.dot_general(amplitude, modes, (((0,), (0,)), ((), ())), precision=highest)

    def jump_lift(amplitude):
        return jump_with(lift(amplitude), move_lifted)

    def absorb(piece):
        amplitude = jnp.einsum("imj,mjc->ic", inverse_view, piece, precision=highest)
        return (amplitude, jnp.sum(piece[:, MODES:], axis=(0, 1)))

    def coarse_solve(right_side, partial_value):
        amplitude, unused = absorb(lax.all_gather(right_side[None], "mod", axis=0, tiled=True))
        total_rho = None if partial_value is None else lax.psum(partial_value, "mod")
        return (amplitude, total_rho)

    def project(values_in, partial_value):
        amplitude, total_rho = coarse_solve(coarse_rhs(orient_flat * values_in), partial_value)
        return (values_in - jump_lift(amplitude), total_rho)

    load_values = loads.astype(jnp.float32)
    first_amplitude, unused_rho = coarse_solve(coarse_rhs(load_values), None)
    multipliers = jump_lift(first_amplitude)
    start = (load_values - orient_flat * multipliers).astype(jnp.bfloat16)
    residual = apply_jump(jnp.dot(start, pinv, preferred_element_type=jnp.float32))
    projected, unused_total = project(residual, None)
    scaled = (orient_flat * projected).astype(jnp.bfloat16)
    smoothed = jnp.dot(scaled, schur, preferred_element_type=jnp.float32)
    partial_value = jnp.sum(scaled.astype(jnp.float32) * smoothed, axis=1)
    corrected, rho = project(apply_jump(smoothed), partial_value)
    lifted = (orient_flat * corrected).astype(jnp.bfloat16)
    response = jnp.dot(lifted, pinv, preferred_element_type=jnp.float32)
    kappa = lax.psum(jnp.sum(lifted.astype(jnp.float32) * response, axis=1), "mod")
    stride = rho / kappa
    multipliers = multipliers + stride[:, None] * corrected
    return multipliers


def solution(mesh):
    in_specs = (
        P(None, "mod"),
        P(None, "mod"),
        P("mod", None),
        P("mod", None),
        P("mod", None),
        P("mod", None, None),
    )
    out_specs = P(None, "mod")
    return jax.shard_map(
        on_device, mesh=mesh, in_specs=in_specs, out_specs=out_specs, check_vma=False
    )
```

profile of v0, /device:TPU:1, one launch (start us, length us, event | category | flops | bytes accessed | tf_op | source)
XLA Modules:
  0.0 439.6 jit_solution(2911055395956350459)
XLA Ops:
  0.9 3.7 reshape.144
  4.6 2.0 copy.8
  6.8 79.2 %all-gather.3 = f32[512,6,32]{2,1,0:T(8,128)S(1)} all-gather(f32[1,6,32]{2,1,0:T(8,128)S(1)} %convolution_bitcast_fusion.22), channel_id=2, replica_groups=mesh['mod'=512] {'mod'}, dimensions={0}, use_global_device_ids=true | all-gather | bytes 393984 | tf_op jit(solution)/shard_map/all_gather | solution.py:69
  87.8 2.1 collective-permute-start
  90.0 3.5 collective-permute-start.1
  95.2 4.0 collective-permute-start.3
  102.6 3.6 collective-permute-start.7
  106.4 3.3 collective-permute-start.4
  109.8 2.2 collective-permute-start.5
  112.0 1.3 collective-permute-start.6
  113.6 3.1 collective-permute-done.6
  117.6 86.2 %all-gather.4 = f32[512,6,32]{2,1,0:T(8,128)S(1)} all-gather(f32[1,6,32]{2,1,0:T(8,128)S(1)} %convolution_bitcast_fusion.21), channel_id=3, replica_groups=mesh['mod'=512] {'mod'}, dimensions={0}, use_global_device_ids=true | all-gather | bytes 393984 | tf_op jit(solution)/shard_map/all_gather | solution.py:69
  207.5 2.1 collective-permute-start.8
  209.6 3.5 collective-permute-start.9
  213.1 1.3 collective-permute-start.10
  214.7 3.1 collective-permute-done.10
  220.1 2.0 collective-permute-start.12
  222.0 3.6 collective-permute-start.13
  226.9 4.0 collective-permute-start.15
  233.2 86.6 %all-gather.5 = f32[512,6,32]{2,1,0:T(8,128)S(1)} all-gather(f32[1,6,32]{2,1,0:T(8,128)S(1)} %convolution_bitcast_fusion.20), channel_id=4, replica_groups=mesh['mod'=512] {'mod'}, dimensions={0}, use_global_device_ids=true | all-gather | bytes 393984 | tf_op jit(solution)/shard_map/all_gather | solution.py:69
  323.5 2.1 collective-permute-start.16
  325.6 3.5 collective-permute-start.17
  330.7 3.1 collective-permute-done.18
  335.1 103.7 %all-reduce = (f32[32]{0:T(128)S(1)}, f32[32]{0:T(128)S(1)}) all-reduce(f32[32]{0:T(128)S(1)} %get-tuple-element.8, f32[32]{0:T(128)S(1)} %fusion.26), channel_id=1, replica_groups=mesh['mod'=512] {'mod'}, use_global_device_ids=true, to_apply=%region_1.0 | all-reduce | flops 64 | bytes 512 | tf_op jit(solution)/shard_map/psum | solution.py:70
  (111 shorter events, 26.0 us)
Async XLA Ops:
  0.0 101.3 %copy-start = (bf16[1024,1024]{1,0:T(8,128)(2,1)S(1)}, bf16[1024,1024]{1,0:T(8,128)(2,1)}, u32[]{:S(2)}) copy-start(bf16[1024,1024]{1,0:T(8,128)(2,1)} %param.8) | copy-start | bytes 6291460
  0.0 6.6 %copy-start.2 = (f32[6,1024]{1,0:T(8,128)S(1)}, f32[6,1024]{1,0:T(8,128)}, u32[]{:S(2)}) copy-start(f32[6,1024]{1,0:T(8,128)} %param.7) | copy-start | bytes 73732
  0.0 6.7 %copy-start.3 = (bf16[32,1024]{1,0:T(8,128)(2,1)S(1)}, bf16[32,1024]{1,0:T(8,128)(2,1)}, u32[]{:S(2)}) copy-start(bf16[32,1024]{1,0:T(8,128)(2,1)} %param.6) | copy-start | bytes 196612
  87.8 13.3 %collective-permute-start = (f32[2,32,128]{2,0,1:T(2,128)S(1)}, f32[2,32,128]{2,0,1:T(2,128)S(1)}, u32[]{:S(2)}, u32[]{:S(2)}) collective-permute-start(f32[2,32,128]{2,0,1:T(2,128)S(1)} %fusion.52), channel_id=1, source_target_pairs={{1,0},{2,1},{3,2},{4,3},{5,4},{6,5},{7,6},{8,7},{9,8},{10,9},{11,1... | collective-permute-start | bytes 98312 | tf_op jit(solution)/shard_map/ppermute | solution.py:15
  90.0 10.7 %collective-permute-start.1 = (f32[2,32,128]{2,0,1:T(2,128)S(1)}, f32[2,32,128]{2,0,1:T(2,128)S(1)}, u32[]{:S(2)}, u32[]{:S(2)}) collective-permute-start(f32[2,32,128]{2,0,1:T(2,128)S(1)} %fusion.57), channel_id=1, source_target_pairs={{0,1},{1,2},{2,3},{3,4},{4,5},{5,6},{6,7},{7,8},{8,9},{9,10},{10,1... | collective-permute-start | bytes 98312 | tf_op jit(solution)/shard_map/ppermute | solution.py:15
  93.7 6.8 %collective-permute-start.2 = (f32[2,32,128]{2,0,1:T(2,128)S(1)}, f32[2,32,128]{2,0,1:T(2,128)S(1)}, u32[]{:S(2)}, u32[]{:S(2)}) collective-permute-start(f32[2,32,128]{2,0,1:T(2,128)S(1)} %fusion.62), channel_id=1, source_target_pairs={{8,0},{9,1},{10,2},{11,3},{12,4},{13,5},{14,6},{15,7},{16,8},{17,9... | collective-permute-start | bytes 98312 | tf_op jit(solution)/shard_map/ppermute | solution.py:15
  95.2 5.0 %collective-permute-start.3 = (f32[2,32,128]{2,0,1:T(2,128)S(1)}, f32[2,32,128]{2,0,1:T(2,128)S(1)}, u32[]{:S(2)}, u32[]{:S(2)}) collective-permute-start(f32[2,32,128]{2,0,1:T(2,128)S(1)} %fusion.67), channel_id=1, source_target_pairs={{0,8},{1,9},{2,10},{3,11},{4,12},{5,13},{6,14},{7,15},{8,16},{9,17... | collective-permute-start | bytes 98312 | tf_op jit(solution)/shard_map/ppermute | solution.py:15
  102.6 10.7 %collective-permute-start.7 = (f32[2,32,128]{2,0,1:T(2,128)S(1)}, f32[2,32,128]{2,0,1:T(2,128)S(1)}, u32[]{:S(2)}, u32[]{:S(2)}) collective-permute-start(f32[2,32,128]{2,0,1:T(2,128)S(1)} %fusion.66), channel_id=1, source_target_pairs={{0,8},{1,9},{2,10},{3,11},{4,12},{5,13},{6,14},{7,15},{8,16},{9,17... | collective-permute-start | bytes 98312 | tf_op jit(solution)/shard_map/ppermute | solution.py:15
  106.4 10.8 %collective-permute-start.4 = (f32[2,32,128]{2,0,1:T(2,128)S(1)}, f32[2,32,128]{2,0,1:T(2,128)S(1)}, u32[]{:S(2)}, u32[]{:S(2)}) collective-permute-start(f32[2,32,128]{2,0,1:T(2,128)S(1)} %fusion.51), channel_id=1, source_target_pairs={{1,0},{2,1},{3,2},{4,3},{5,4},{6,5},{7,6},{8,7},{9,8},{10,9},{11,1... | collective-permute-start | bytes 98312 | tf_op jit(solution)/shard_map/ppermute | solution.py:15
  109.8 7.2 %collective-permute-start.5 = (f32[2,32,128]{2,0,1:T(2,128)S(1)}, f32[2,32,128]{2,0,1:T(2,128)S(1)}, u32[]{:S(2)}, u32[]{:S(2)}) collective-permute-start(f32[2,32,128]{2,0,1:T(2,128)S(1)} %fusion.56), channel_id=1, source_target_pairs={{0,1},{1,2},{2,3},{3,4},{4,5},{5,6},{6,7},{7,8},{8,9},{9,10},{10,1... | collective-permute-start | bytes 98312 | tf_op jit(solution)/shard_map/ppermute | solution.py:15
  112.0 4.7 %collective-permute-start.6 = (f32[2,32,128]{2,0,1:T(2,128)S(1)}, f32[2,32,128]{2,0,1:T(2,128)S(1)}, u32[]{:S(2)}, u32[]{:S(2)}) collective-permute-start(f32[2,32,128]{2,0,1:T(2,128)S(1)} %fusion.61), channel_id=1, source_target_pairs={{8,0},{9,1},{10,2},{11,3},{12,4},{13,5},{14,6},{15,7},{16,8},{17,9... | collective-permute-start | bytes 98312 | tf_op jit(solution)/shard_map/ppermute | solution.py:15
  204.9 13.7 %copy-start.1 = (bf16[1024,1024]{1,0:T(8,128)(2,1)S(1)}, bf16[1024,1024]{1,0:T(8,128)(2,1)}, u32[]{:S(2)}) copy-start(bf16[1024,1024]{1,0:T(8,128)(2,1)} %param.9) | copy-start | bytes 6291460
  206.0 8.4 %collective-permute-start.11 = (f32[2,32,128]{2,0,1:T(2,128)S(1)}, f32[2,32,128]{2,0,1:T(2,128)S(1)}, u32[]{:S(2)}, u32[]{:S(2)}) collective-permute-start(f32[2,32,128]{2,0,1:T(2,128)S(1)} %fusion.65), channel_id=1, source_target_pairs={{0,8},{1,9},{2,10},{3,11},{4,12},{5,13},{6,14},{7,15},{8,16},{9,17... | collective-permute-start | bytes 98312 | tf_op jit(solution)/shard_map/ppermute | solution.py:15
  207.5 10.8 %collective-permute-start.8 = (f32[2,32,128]{2,0,1:T(2,128)S(1)}, f32[2,32,128]{2,0,1:T(2,128)S(1)}, u32[]{:S(2)}, u32[]{:S(2)}) collective-permute-start(f32[2,32,128]{2,0,1:T(2,128)S(1)} %fusion.50), channel_id=1, source_target_pairs={{1,0},{2,1},{3,2},{4,3},{5,4},{6,5},{7,6},{8,7},{9,8},{10,9},{11,1... | collective-permute-start | bytes 98312 | tf_op jit(solution)/shard_map/ppermute | solution.py:15
  209.6 8.4 %collective-permute-start.9 = (f32[2,32,128]{2,0,1:T(2,128)S(1)}, f32[2,32,128]{2,0,1:T(2,128)S(1)}, u32[]{:S(2)}, u32[]{:S(2)}) collective-permute-start(f32[2,32,128]{2,0,1:T(2,128)S(1)} %fusion.55), channel_id=1, source_target_pairs={{0,1},{1,2},{2,3},{3,4},{4,5},{5,6},{6,7},{7,8},{8,9},{9,10},{10,1... | collective-permute-start | bytes 98312 | tf_op jit(solution)/shard_map/ppermute | solution.py:15
  213.1 4.7 %collective-permute-start.10 = (f32[2,32,128]{2,0,1:T(2,128)S(1)}, f32[2,32,128]{2,0,1:T(2,128)S(1)}, u32[]{:S(2)}, u32[]{:S(2)}) collective-permute-start(f32[2,32,128]{2,0,1:T(2,128)S(1)} %fusion.60), channel_id=1, source_target_pairs={{8,0},{9,1},{10,2},{11,3},{12,4},{13,5},{14,6},{15,7},{16,8},{17,9... | collective-permute-start | bytes 98312 | tf_op jit(solution)/shard_map/ppermute | solution.py:15
  220.1 12.7 %collective-permute-start.12 = (f32[2,32,128]{2,0,1:T(2,128)S(1)}, f32[2,32,128]{2,0,1:T(2,128)S(1)}, u32[]{:S(2)}, u32[]{:S(2)}) collective-permute-start(f32[2,32,128]{2,0,1:T(2,128)S(1)} %fusion.49), channel_id=1, source_target_pairs={{1,0},{2,1},{3,2},{4,3},{5,4},{6,5},{7,6},{8,7},{9,8},{10,9},{11,1... | collective-permute-start | bytes 98312 | tf_op jit(solution)/shard_map/ppermute | solution.py:15
  222.0 10.4 %collective-permute-start.13 = (f32[2,32,128]{2,0,1:T(2,128)S(1)}, f32[2,32,128]{2,0,1:T(2,128)S(1)}, u32[]{:S(2)}, u32[]{:S(2)}) collective-permute-start(f32[2,32,128]{2,0,1:T(2,128)S(1)} %fusion.54), channel_id=1, source_target_pairs={{0,1},{1,2},{2,3},{3,4},{4,5},{5,6},{6,7},{7,8},{8,9},{9,10},{10,1... | collective-permute-start | bytes 98312 | tf_op jit(solution)/shard_map/ppermute | solution.py:15
  225.6 6.6 %collective-permute-start.14 = (f32[2,32,128]{2,0,1:T(2,128)S(1)}, f32[2,32,128]{2,0,1:T(2,128)S(1)}, u32[]{:S(2)}, u32[]{:S(2)}) collective-permute-start(f32[2,32,128]{2,0,1:T(2,128)S(1)} %fusion.59), channel_id=1, source_target_pairs={{8,0},{9,1},{10,2},{11,3},{12,4},{13,5},{14,6},{15,7},{16,8},{17,9... | collective-permute-start | bytes 98312 | tf_op jit(solution)/shard_map/ppermute | solution.py:15
  226.9 5.0 %collective-permute-start.15 = (f32[2,32,128]{2,0,1:T(2,128)S(1)}, f32[2,32,128]{2,0,1:T(2,128)S(1)}, u32[]{:S(2)}, u32[]{:S(2)}) collective-permute-start(f32[2,32,128]{2,0,1:T(2,128)S(1)} %fusion.64), channel_id=1, source_target_pairs={{0,8},{1,9},{2,10},{3,11},{4,12},{5,13},{6,14},{7,15},{8,16},{9,17... | collective-permute-start | bytes 98312 | tf_op jit(solution)/shard_map/ppermute | solution.py:15
  322.0 8.4 %collective-permute-start.19 = (f32[2,32,128]{2,0,1:T(2,128)S(1)}, f32[2,32,128]{2,0,1:T(2,128)S(1)}, u32[]{:S(2)}, u32[]{:S(2)}) collective-permute-start(f32[2,32,128]{2,0,1:T(2,128)S(1)} %fusion.63), channel_id=1, source_target_pairs={{0,8},{1,9},{2,10},{3,11},{4,12},{5,13},{6,14},{7,15},{8,16},{9,17... | collective-permute-start | bytes 98312 | tf_op jit(solution)/shard_map/ppermute | solution.py:15
  323.5 10.8 %collective-permute-start.16 = (f32[2,32,128]{2,0,1:T(2,128)S(1)}, f32[2,32,128]{2,0,1:T(2,128)S(1)}, u32[]{:S(2)}, u32[]{:S(2)}) collective-permute-start(f32[2,32,128]{2,0,1:T(2,128)S(1)} %fusion.48), channel_id=1, source_target_pairs={{1,0},{2,1},{3,2},{4,3},{5,4},{6,5},{7,6},{8,7},{9,8},{10,9},{11,1... | collective-permute-start | bytes 98312 | tf_op jit(solution)/shard_map/ppermute | solution.py:15
  325.6 8.4 %collective-permute-start.17 = (f32[2,32,128]{2,0,1:T(2,128)S(1)}, f32[2,32,128]{2,0,1:T(2,128)S(1)}, u32[]{:S(2)}, u32[]{:S(2)}) collective-permute-start(f32[2,32,128]{2,0,1:T(2,128)S(1)} %fusion.53), channel_id=1, source_target_pairs={{0,1},{1,2},{2,3},{3,4},{4,5},{5,6},{6,7},{7,8},{8,9},{9,10},{10,1... | collective-permute-start | bytes 98312 | tf_op jit(solution)/shard_map/ppermute | solution.py:15
  329.1 4.7 %collective-permute-start.18 = (f32[2,32,128]{2,0,1:T(2,128)S(1)}, f32[2,32,128]{2,0,1:T(2,128)S(1)}, u32[]{:S(2)}, u32[]{:S(2)}) collective-permute-start(f32[2,32,128]{2,0,1:T(2,128)S(1)} %fusion.58), channel_id=1, source_target_pairs={{8,0},{9,1},{10,2},{11,3},{12,4},{13,5},{14,6},{15,7},{16,8},{17,9... | collective-permute-start | bytes 98312 | tf_op jit(solution)/shard_map/ppermute | solution.py:15
where the time goes:
time: 440 us
  blocking collectives  356 us (81%)
  starting transfers between devices  48.5 us (11%)
  matrix products  15.1 us (3%)
  waiting for transfers between devices  11.1 us (3%)
  local copies, waits for them, and re-layouts  6.04 us (1%)
    all_gather x3, blocking collectives, coarse_solve(): lax.all_gather(right_side[None], 'mod', axis=0, tiled=True)  252 us
    psum x1, blocking collectives, coarse_solve(): lax.psum(partial_value, 'mod')  104 us
    ppermute x20, starting transfers between devices, shifted(): return lax.ppermute(block, axis, route)  48.5 us
    ppermute x20, waiting for transfers between devices, shifted(): return lax.ppermute(block, axis, route)  11.1 us
  transfers between devices with their start and end apart: 20, of which 5 were waited for; matrix products, arithmetic and copies ran while one was open for 1% of the time, Pallas kernels for 0%

commit v1 on v0

--- a/solution.py
+++ b/solution.py
@@ -7,6 +7,10 @@
 MAXC = 2
 ACROSS = 8
 highest = lax.Precision.HIGHEST
+
+
+def start_spot(x0):
+    return jax.lax.all_gather(x0, "mod").sum(axis=0)
 
 
 def shifted(block, axis, distance):
@@ -67,7 +71,7 @@
 
     def coarse_solve(right_side, partial_value):
         amplitude, unused = absorb(lax.all_gather(right_side[None], "mod", axis=0, tiled=True))
-        total_rho = None if partial_value is None else lax.psum(partial_value, "mod")
+        total_rho = None if partial_value is None else start_spot(partial_value)
         return (amplitude, total_rho)
 
     def project(values_in, partial_value):

time: 440 us -> 704 us (1.60)
  waiting for transfers between devices: 11.1 us -> 279 us
  blocking collectives: 356 us -> 338 us
  between operations: 0.82 us -> 14.2 us
    unnamed x0 -> x2, waiting for transfers between devices: none -> 273 us
    all_gather x3, blocking collectives: 252 us -> 235 us  [coarse_solve(): lax.all_gather(right_side[None], 'mod', axis=0, tiled=True)]
  transfers between devices with their start and end apart: 20 -> 21, of which waited for: 5 -> 5; matrix products, arithmetic and copies ran while one was open for 1% -> 1% of each run, Pallas kernels for 0% -> 0%
where the time goes in v1:
time: 704 us; the launch traced here: 703 us
  blocking collectives  338 us (48%)
  waiting for transfers between devices  279 us (40%)
  starting transfers between devices  46.6 us (7%)
  matrix products  15.1 us (2%)
  between operations  14.2 us (2%)
  local copies, waits for them, and re-layouts  7.89 us (1%)
    unnamed x2, waiting for transfers between devices  273 us
    all_gather x3, blocking collectives, coarse_solve(): lax.all_gather(right_side[None], 'mod', axis=0, tiled=True)  235 us
    psum x1, blocking collectives, on_device(): lax.psum(jnp.sum(lifted.astype(jnp.float32) * response, axis=1), 'mod')  103 us
    ppermute x20, starting transfers between devices, shifted(): return lax.ppermute(block, axis, route)  46.6 us
  transfers between devices with their start and end apart: 21, of which 5 were waited for; matrix products, arithmetic and copies ran while one was open for 1% of the time, Pallas kernels for 0%

profile of v1, /device:TPU:1, one launch (start us, length us, event | category | flops | bytes accessed | tf_op | source)
XLA Modules:
  0.0 703.1 jit_solution(1641483591612411337)
XLA Ops:
  7.5 3.6 reshape.144
  11.1 2.0 copy.8
  13.3 79.2 %all-gather.4 = f32[512,6,32]{2,1,0:T(8,128)S(1)} all-gather(f32[1,6,32]{2,1,0:T(8,128)S(1)} %convolution_bitcast_fusion.22), channel_id=2, replica_groups=mesh['mod'=512] {'mod'}, dimensions={0}, use_global_device_ids=true | all-gather | bytes 393984 | tf_op jit(solution)/shard_map/all_gather | solution.py:73
  95.8 2.4 collective-permute-start.1
  98.3 4.3 collective-permute-start.3
  102.8 2.0 collective-permute-start
  105.7 2.3 collective-permute-done
  109.6 1.9 collective-permute-start.7
  112.9 2.2 collective-permute-start.5
  115.1 3.6 collective-permute-start.4
  120.8 86.7 %all-gather.5 = f32[512,6,32]{2,1,0:T(8,128)S(1)} all-gather(f32[1,6,32]{2,1,0:T(8,128)S(1)} %convolution_bitcast_fusion.21), channel_id=3, replica_groups=mesh['mod'=512] {'mod'}, dimensions={0}, use_global_device_ids=true | all-gather | bytes 393984 | tf_op jit(solution)/shard_map/all_gather | solution.py:73
  209.7 1.9 collective-permute-start.9
  212.9 4.0 collective-permute-start.11
  216.9 3.0 collective-permute-start.8
  223.9 1.9 collective-permute-start.15
  227.2 2.2 collective-permute-start.13
  229.4 2.3 collective-permute-start.12
  232.8 272.8 %all-reduce.3.cloned.1.call-done = f32[16384]{0:T(1024)} async-done(((f32[16384]{0:T(1024)}), f32[16384]{0:T(1024)}) %all-reduce.3.cloned.1.call-update) | async-done | bytes 65552
  507.8 69.1 %all-gather.6 = f32[512,6,32]{2,1,0:T(8,128)S(1)} all-gather(f32[1,6,32]{2,1,0:T(8,128)S(1)} %convolution_bitcast_fusion.20), channel_id=5, replica_groups=mesh['mod'=512] {'mod'}, dimensions={0}, use_global_device_ids=true | all-gather | bytes 393984 | tf_op jit(solution)/shard_map/all_gather | solution.py:73
  580.5 1.9 collective-permute-start.17
  582.4 4.0 collective-permute-start.19
  586.4 2.7 collective-permute-start.16
  590.1 1.6 collective-permute-done.16
  592.6 102.9 %psum.7 = f32[32]{0:T(128)S(1)} all-reduce(f32[32]{0:T(128)S(1)} %fusion.26), channel_id=1, replica_groups=mesh['mod'=512] {'mod'}, use_global_device_ids=true, to_apply=%region_3.0 | all-reduce | flops 32 | bytes 256 | tf_op jit(solution)/shard_map/psum | solution.py:93
  (120 shorter events, 28.3 us)
Async XLA Ops:
  6.5 101.8 %copy-start = (bf16[1024,1024]{1,0:T(8,128)(2,1)S(1)}, bf16[1024,1024]{1,0:T(8,128)(2,1)}, u32[]{:S(2)}) copy-start(bf16[1024,1024]{1,0:T(8,128)(2,1)} %param.8) | copy-start | bytes 6291460
  6.5 6.6 copy-start.2
  6.5 499.0 %all-reduce.3.cloned.1.call-start = ((), (), s32[]{:S(2)}) async-start(), calls=%async_computation | async-start | bytes 131072
  94.3 10.6 %collective-permute-start.2 = (f32[2,32,128]{2,0,1:T(2,128)S(1)}, f32[2,32,128]{2,0,1:T(2,128)S(1)}, u32[]{:S(2)}, u32[]{:S(2)}) collective-permute-start(f32[2,32,128]{2,0,1:T(2,128)S(1)} %fusion.62), channel_id=1, source_target_pairs={{8,0},{9,1},{10,2},{11,3},{12,4},{13,5},{14,6},{15,7},{16,8},{17,9... | collective-permute-start | bytes 98312 | tf_op jit(solution)/shard_map/ppermute | solution.py:19
  95.8 9.4 %collective-permute-start.1 = (f32[2,32,128]{2,0,1:T(2,128)S(1)}, f32[2,32,128]{2,0,1:T(2,128)S(1)}, u32[]{:S(2)}, u32[]{:S(2)}) collective-permute-start(f32[2,32,128]{2,0,1:T(2,128)S(1)} %fusion.57), channel_id=1, source_target_pairs={{0,1},{1,2},{2,3},{3,4},{4,5},{5,6},{6,7},{7,8},{8,9},{9,10},{10,1... | collective-permute-start | bytes 98312 | tf_op jit(solution)/shard_map/ppermute | solution.py:19
  98.3 7.1 %collective-permute-start.3 = (f32[2,32,128]{2,0,1:T(2,128)S(1)}, f32[2,32,128]{2,0,1:T(2,128)S(1)}, u32[]{:S(2)}, u32[]{:S(2)}) collective-permute-start(f32[2,32,128]{2,0,1:T(2,128)S(1)} %fusion.67), channel_id=1, source_target_pairs={{0,8},{1,9},{2,10},{3,11},{4,12},{5,13},{6,14},{7,15},{8,16},{9,17... | collective-permute-start | bytes 98312 | tf_op jit(solution)/shard_map/ppermute | solution.py:19
  102.8 5.2 collective-permute-start
  109.6 9.1 %collective-permute-start.7 = (f32[2,32,128]{2,0,1:T(2,128)S(1)}, f32[2,32,128]{2,0,1:T(2,128)S(1)}, u32[]{:S(2)}, u32[]{:S(2)}) collective-permute-start(f32[2,32,128]{2,0,1:T(2,128)S(1)} %fusion.66), channel_id=1, source_target_pairs={{0,8},{1,9},{2,10},{3,11},{4,12},{5,13},{6,14},{7,15},{8,16},{9,17... | collective-permute-start | bytes 98312 | tf_op jit(solution)/shard_map/ppermute | solution.py:19
  111.6 7.5 %collective-permute-start.6 = (f32[2,32,128]{2,0,1:T(2,128)S(1)}, f32[2,32,128]{2,0,1:T(2,128)S(1)}, u32[]{:S(2)}, u32[]{:S(2)}) collective-permute-start(f32[2,32,128]{2,0,1:T(2,128)S(1)} %fusion.61), channel_id=1, source_target_pairs={{8,0},{9,1},{10,2},{11,3},{12,4},{13,5},{14,6},{15,7},{16,8},{17,9... | collective-permute-start | bytes 98312 | tf_op jit(solution)/shard_map/ppermute | solution.py:19
  112.9 6.4 collective-permute-start.5
  115.1 5.2 collective-permute-start.4
  208.5 14.0 %copy-start.1 = (bf16[1024,1024]{1,0:T(8,128)(2,1)S(1)}, bf16[1024,1024]{1,0:T(8,128)(2,1)}, u32[]{:S(2)}) copy-start(bf16[1024,1024]{1,0:T(8,128)(2,1)} %param.9) | copy-start | bytes 6291460
  209.7 10.3 %collective-permute-start.9 = (f32[2,32,128]{2,0,1:T(2,128)S(1)}, f32[2,32,128]{2,0,1:T(2,128)S(1)}, u32[]{:S(2)}, u32[]{:S(2)}) collective-permute-start(f32[2,32,128]{2,0,1:T(2,128)S(1)} %fusion.55), channel_id=1, source_target_pairs={{0,1},{1,2},{2,3},{3,4},{4,5},{5,6},{6,7},{7,8},{8,9},{9,10},{10,1... | collective-permute-start | bytes 98312 | tf_op jit(solution)/shard_map/ppermute | solution.py:19
  211.6 8.7 %collective-permute-start.10 = (f32[2,32,128]{2,0,1:T(2,128)S(1)}, f32[2,32,128]{2,0,1:T(2,128)S(1)}, u32[]{:S(2)}, u32[]{:S(2)}) collective-permute-start(f32[2,32,128]{2,0,1:T(2,128)S(1)} %fusion.60), channel_id=1, source_target_pairs={{8,0},{9,1},{10,2},{11,3},{12,4},{13,5},{14,6},{15,7},{16,8},{17,9... | collective-permute-start | bytes 98312 | tf_op jit(solution)/shard_map/ppermute | solution.py:19
  212.9 7.6 %collective-permute-start.11 = (f32[2,32,128]{2,0,1:T(2,128)S(1)}, f32[2,32,128]{2,0,1:T(2,128)S(1)}, u32[]{:S(2)}, u32[]{:S(2)}) collective-permute-start(f32[2,32,128]{2,0,1:T(2,128)S(1)} %fusion.65), channel_id=1, source_target_pairs={{0,8},{1,9},{2,10},{3,11},{4,12},{5,13},{6,14},{7,15},{8,16},{9,17... | collective-permute-start | bytes 98312 | tf_op jit(solution)/shard_map/ppermute | solution.py:19
  216.9 5.2 collective-permute-start.8
  223.9 282.6 %collective-permute-start.15 = (f32[2,32,128]{2,0,1:T(2,128)S(1)}, f32[2,32,128]{2,0,1:T(2,128)S(1)}, u32[]{:S(2)}, u32[]{:S(2)}) collective-permute-start(f32[2,32,128]{2,0,1:T(2,128)S(1)} %fusion.64), channel_id=1, source_target_pairs={{0,8},{1,9},{2,10},{3,11},{4,12},{5,13},{6,14},{7,15},{8,16},{9,17... | collective-permute-start | bytes 98312 | tf_op jit(solution)/shard_map/ppermute | solution.py:19
  225.9 281.0 %collective-permute-start.14 = (f32[2,32,128]{2,0,1:T(2,128)S(1)}, f32[2,32,128]{2,0,1:T(2,128)S(1)}, u32[]{:S(2)}, u32[]{:S(2)}) collective-permute-start(f32[2,32,128]{2,0,1:T(2,128)S(1)} %fusion.59), channel_id=1, source_target_pairs={{8,0},{9,1},{10,2},{11,3},{12,4},{13,5},{14,6},{15,7},{16,8},{17,9... | collective-permute-start | bytes 98312 | tf_op jit(solution)/shard_map/ppermute | solution.py:19
  227.2 279.9 %collective-permute-start.13 = (f32[2,32,128]{2,0,1:T(2,128)S(1)}, f32[2,32,128]{2,0,1:T(2,128)S(1)}, u32[]{:S(2)}, u32[]{:S(2)}) collective-permute-start(f32[2,32,128]{2,0,1:T(2,128)S(1)} %fusion.54), channel_id=1, source_target_pairs={{0,1},{1,2},{2,3},{3,4},{4,5},{5,6},{6,7},{7,8},{8,9},{9,10},{10,1... | collective-permute-start | bytes 98312 | tf_op jit(solution)/shard_map/ppermute | solution.py:19
  229.4 278.0 %collective-permute-start.12 = (f32[2,32,128]{2,0,1:T(2,128)S(1)}, f32[2,32,128]{2,0,1:T(2,128)S(1)}, u32[]{:S(2)}, u32[]{:S(2)}) collective-permute-start(f32[2,32,128]{2,0,1:T(2,128)S(1)} %fusion.49), channel_id=1, source_target_pairs={{1,0},{2,1},{3,2},{4,3},{5,4},{6,5},{7,6},{8,7},{9,8},{10,9},{11,1... | collective-permute-start | bytes 98312 | tf_op jit(solution)/shard_map/ppermute | solution.py:19
  579.2 10.0 %collective-permute-start.18 = (f32[2,32,128]{2,0,1:T(2,128)S(1)}, f32[2,32,128]{2,0,1:T(2,128)S(1)}, u32[]{:S(2)}, u32[]{:S(2)}) collective-permute-start(f32[2,32,128]{2,0,1:T(2,128)S(1)} %fusion.58), channel_id=1, source_target_pairs={{8,0},{9,1},{10,2},{11,3},{12,4},{13,5},{14,6},{15,7},{16,8},{17,9... | collective-permute-start | bytes 98312 | tf_op jit(solution)/shard_map/ppermute | solution.py:19
  580.5 9.0 %collective-permute-start.17 = (f32[2,32,128]{2,0,1:T(2,128)S(1)}, f32[2,32,128]{2,0,1:T(2,128)S(1)}, u32[]{:S(2)}, u32[]{:S(2)}) collective-permute-start(f32[2,32,128]{2,0,1:T(2,128)S(1)} %fusion.53), channel_id=1, source_target_pairs={{0,1},{1,2},{2,3},{3,4},{4,5},{5,6},{6,7},{7,8},{8,9},{9,10},{10,1... | collective-permute-start | bytes 98312 | tf_op jit(solution)/shard_map/ppermute | solution.py:19
  582.4 7.4 %collective-permute-start.19 = (f32[2,32,128]{2,0,1:T(2,128)S(1)}, f32[2,32,128]{2,0,1:T(2,128)S(1)}, u32[]{:S(2)}, u32[]{:S(2)}) collective-permute-start(f32[2,32,128]{2,0,1:T(2,128)S(1)} %fusion.63), channel_id=1, source_target_pairs={{0,8},{1,9},{2,10},{3,11},{4,12},{5,13},{6,14},{7,15},{8,16},{9,17... | collective-permute-start | bytes 98312 | tf_op jit(solution)/shard_map/ppermute | solution.py:19
  586.4 5.2 collective-permute-start.16
  (2 other events, 7.3 us)
Sparse Core Ops, SparseCore 0:
  232.8 272.7 all-reduce.2
